TPU v7x, 256 devices: a whole 4x4x8 slice. The times are simulated.
256 devices in a mesh: dp: 2 (over core), expert: 128 (over z, x, y).
Axes of the slice: x: 4, y: 4, z: 8, core: 2. Of those that a mesh axis runs over, the one named last changes fastest.
Arguments:
- out_grad: bfloat16 [16384, 1024], P(('dp', 'expert')), may hold values from -6 to 6
- layer_input: bfloat16 [16384, 1024], P(('dp', 'expert')), may hold values from -6 to 6
- combine: float32 [16384, 8], P(('dp', 'expert')), may hold values from 0.05 to 0.5
- routes: int32 [16384, 8], P(('dp', 'expert')), may hold values from 0 to 127, all different within a row; in each aligned block of 64 rows (0 to 63, 64 to 127, ...) at most 8 rows name the same one
- w_gate_up: bfloat16 [128, 1024, 768], P('expert'), may hold values from -0.1875 to 0.1875
- w_down: bfloat16 [128, 384, 1024], P('expert'), may hold values from -0.3125 to 0.3125
- m_gate_up: float32 [128, 1024, 768], P('expert', 'dp'), may hold values from -0.75 to 0.75
- v_gate_up: float32 [128, 1024, 768], P('expert', 'dp'), may hold values from 0.001 to 0.1
- m_down: float32 [128, 384, 1024], P('expert', None, 'dp'), may hold values from -0.75 to 0.75
- v_down: float32 [128, 384, 1024], P('expert', None, 'dp'), may hold values from 0.001 to 0.1
- swap_pairs: int32 [32, 2], replicated, may hold values from 0 to 127, as said below
Outputs:
- in_grad: bfloat16 [16384, 1024], P(('dp', 'expert'))
- new_gate_up: bfloat16 [128, 1024, 768], P('expert', 'dp')
- new_down: bfloat16 [128, 384, 1024], P('expert', None, 'dp')
- new_m_gate_up: float32 [128, 1024, 768], P('expert', 'dp')
- new_v_gate_up: float32 [128, 1024, 768], P('expert', 'dp')
- new_m_down: float32 [128, 384, 1024], P('expert', None, 'dp')
- new_v_down: float32 [128, 384, 1024], P('expert', None, 'dp')
Inputs may be any that keep to these rules, and one draw needn't show every extreme that they name: `routes`: each row names 8 different experts; among the rows of one device no expert is named more than 8 times, a bound that some block reaches. `swap_pairs`: no device appears twice in the list; devices 0 and 127 are always in it.
All inputs are finite; a program needn't handle non-finite values. Where the computation divides by a largest or mean magnitude, that divisor is 1e-20 or more.
Results may differ from a plain program's by a relative error of at most 0.0064.
Values may be sent and summed in bfloat16 or wider, within the bound.
A program may use at most 128 MiB of HBM per device.

v0:
```python
import jax
import jax.numpy as jnp
from jax import lax
from jax.sharding import PartitionSpec as P

BETA_ONE = 0.9
BETA_TWO = 0.95
RATE = 0.001
DECAY = 0.1
ADAM_EPS = 1e-08
PEAK_EPS = 1e-06


def partner_table(swap_pairs, expert_count):
    devices = jnp.arange(expert_count, dtype=jnp.int32)
    first_dev = swap_pairs[:, 0]
    second_dev = swap_pairs[:, 1]
    hit_first = devices[:, None] == first_dev[None, :]
    hit_second = devices[:, None] == second_dev[None, :]
    other = jnp.sum(
        jnp.where(hit_first, second_dev[None, :], 0) + jnp.where(hit_second, first_dev[None, :], 0),
        axis=1,
    )
    paired = jnp.any(hit_first | hit_second, axis=1)
    return jnp.where(paired, other, devices)


def slot_ranks(route_ids, expert_count):
    flat_ids = route_ids.reshape(-1)
    onehot = (flat_ids[:, None] == jnp.arange(expert_count, dtype=jnp.int32)[None, :]).astype(
        jnp.int32
    )
    before = jnp.cumsum(onehot, axis=0) - onehot
    return jnp.sum(before * onehot, axis=1)


def expert_backward(slot_grad, slot_input, gate_up, down_proj):
    hidden_units = down_proj.shape[0]
    pre_act = jnp.dot(slot_input, gate_up, preferred_element_type=jnp.float32)
    gate_pre = pre_act[:, :hidden_units]
    up_pre = pre_act[:, hidden_units:]
    sigmoid_gate = jax.nn.sigmoid(gate_pre)
    gate_act = gate_pre * sigmoid_gate
    hidden = (gate_act * up_pre).astype(jnp.bfloat16)
    d_hidden = lax.dot_general(
        slot_grad, down_proj, (((1,), (1,)), ((), ())), preferred_element_type=jnp.float32
    )
    d_gate = d_hidden * up_pre * sigmoid_gate * (1.0 + gate_pre * (1.0 - sigmoid_gate))
    d_up = d_hidden * gate_act
    d_pre = jnp.concatenate([d_gate, d_up], axis=1).astype(jnp.bfloat16)
    grad_down = lax.dot_general(
        hidden, slot_grad, (((0,), (0,)), ((), ())), preferred_element_type=jnp.float32
    )
    grad_gate_up = lax.dot_general(
        slot_input, d_pre, (((0,), (0,)), ((), ())), preferred_element_type=jnp.float32
    )
    slot_back = lax.dot_general(
        d_pre, gate_up, (((1,), (1,)), ((), ())), preferred_element_type=jnp.float32
    ).astype(jnp.bfloat16)
    return (slot_back, grad_gate_up, grad_down)


def adam_update(weight, grad, mean_in, square_in, scale_by):
    scaled = grad * scale_by
    mean_new = BETA_ONE * mean_in + (1.0 - BETA_ONE) * scaled
    square_new = BETA_TWO * square_in + (1.0 - BETA_TWO) * scaled * scaled
    weight_wide = weight.astype(jnp.float32)
    step_size = mean_new / (jnp.sqrt(square_new) + ADAM_EPS)
    weight_new = (weight_wide - RATE * (step_size + DECAY * weight_wide)).astype(jnp.bfloat16)
    return (weight_new, mean_new, square_new)


def move_moments(gate_mean, gate_square, down_mean, down_square, partner):
    expert_count = partner.shape[0]
    spread_out = (
        lax.all_to_all(
            gate_mean.reshape(1, expert_count, -1),
            "expert",
            split_axis=1,
            concat_axis=0,
            tiled=True,
        ),
        lax.all_to_all(
            gate_square.reshape(1, expert_count, -1),
            "expert",
            split_axis=1,
            concat_axis=0,
            tiled=True,
        ),
        lax.all_to_all(
            down_mean.reshape(1, expert_count, -1),
            "expert",
            split_axis=1,
            concat_axis=0,
            tiled=True,
        ),
        lax.all_to_all(
            down_square.reshape(1, expert_count, -1),
            "expert",
            split_axis=1,
            concat_axis=0,
            tiled=True,
        ),
    )
    picked = [jnp.take(element, partner, axis=0) for element in spread_out]
    arrived = (
        lax.all_to_all(picked[0], "expert", split_axis=0, concat_axis=1, tiled=True),
        lax.all_to_all(picked[1], "expert", split_axis=0, concat_axis=1, tiled=True),
        lax.all_to_all(picked[2], "expert", split_axis=0, concat_axis=1, tiled=True),
        lax.all_to_all(picked[3], "expert", split_axis=0, concat_axis=1, tiled=True),
    )
    return (
        arrived[0].reshape(gate_mean.shape),
        arrived[1].reshape(gate_square.shape),
        arrived[2].reshape(down_mean.shape),
        arrived[3].reshape(down_square.shape),
    )


def move_weights_after(gate_up, down_proj, partner):
    expert_count = partner.shape[0]
    spread_out = (
        lax.all_to_all(
            gate_up.reshape(1, expert_count, -1), "expert", split_axis=1, concat_axis=0, tiled=True
        ),
        lax.all_to_all(
            down_proj.reshape(1, expert_count, -1),
            "expert",
            split_axis=1,
            concat_axis=0,
            tiled=True,
        ),
    )
    picked = [jnp.take(element, partner, axis=0) for element in spread_out]
    arrived = (
        lax.all_to_all(picked[0], "expert", split_axis=0, concat_axis=1, tiled=True),
        lax.all_to_all(picked[1], "expert", split_axis=0, concat_axis=1, tiled=True),
    )
    return (arrived[0].reshape(gate_up.shape), arrived[1].reshape(down_proj.shape))


def per_device(
    out_grad,
    layer_input,
    combine,
    routes,
    w_gate_up,
    w_down,
    m_gate_up,
    v_gate_up,
    m_down,
    v_down,
    swap_pairs,
):
    expert_count = lax.axis_size("expert")
    replicas = lax.axis_size("dp")
    replica = lax.axis_index("dp")
    partner = partner_table(swap_pairs, expert_count)
    tok_rows, top_count = routes.shape
    capacity = 2 * tok_rows * top_count // expert_count
    model_width = out_grad.shape[1]
    ranks = slot_ranks(routes, expert_count)
    assign = tok_rows * top_count
    slot_place = routes.reshape(-1) * capacity + ranks
    slot_owner = (
        jnp.full((expert_count * capacity,), -1, jnp.int32)
        .at[slot_place]
        .set(jnp.arange(assign, dtype=jnp.int32))
    )
    is_live = slot_owner >= 0
    safe_index = jnp.maximum(slot_owner, 0)
    token_ids = safe_index // top_count
    weights = jnp.where(is_live, combine.reshape(-1)[safe_index], jnp.float32(0.0))
    slot_grad = (out_grad[token_ids].astype(jnp.float32) * weights[:, None]).astype(jnp.bfloat16)
    slot_input = jnp.where(is_live[:, None], layer_input[token_ids], jnp.zeros((), jnp.bfloat16))
    slot_grad, slot_input = (
        lax.all_to_all(
            slot_grad.reshape(expert_count, capacity, model_width),
            "expert",
            split_axis=0,
            concat_axis=0,
            tiled=True,
        ),
        lax.all_to_all(
            slot_input.reshape(expert_count, capacity, model_width),
            "expert",
            split_axis=0,
            concat_axis=0,
            tiled=True,
        ),
    )
    slot_back, grad_gate_up, grad_down = expert_backward(
        slot_grad.reshape(-1, model_width),
        slot_input.reshape(-1, model_width),
        w_gate_up[0],
        w_down[0],
    )
    slot_back = lax.all_to_all(
        slot_back.reshape(expert_count, capacity, model_width),
        "expert",
        split_axis=0,
        concat_axis=0,
        tiled=True,
    )
    returned = slot_back.reshape(expert_count * capacity, model_width)[slot_place].reshape(
        tok_rows, top_count, model_width
    )
    in_grad = jnp.sum(returned, axis=1, dtype=jnp.float32).astype(jnp.bfloat16)
    half_rows = model_width // replicas
    part_gate_up, part_down = (
        lax.psum_scatter(
            grad_gate_up.astype(jnp.bfloat16), "dp", scatter_dimension=0, tiled=True
        ).astype(jnp.float32),
        lax.psum_scatter(
            grad_down.astype(jnp.bfloat16), "dp", scatter_dimension=1, tiled=True
        ).astype(jnp.float32),
    )
    local_peak = jnp.maximum(jnp.max(jnp.abs(part_gate_up)), jnp.max(jnp.abs(part_down)))
    peak_abs = lax.pmax(local_peak, "dp")
    scale_by = 1.0 / (peak_abs + PEAK_EPS)
    own_gate_up = lax.dynamic_slice_in_dim(w_gate_up[0], replica * half_rows, half_rows, 0)
    own_down = lax.dynamic_slice_in_dim(w_down[0], replica * half_rows, half_rows, 1)
    new_gu, gate_mean, gate_square = adam_update(
        own_gate_up, part_gate_up, m_gate_up[0], v_gate_up[0], scale_by
    )
    new_dn, down_mean, down_square = adam_update(
        own_down, part_down, m_down[0], v_down[0], scale_by
    )
    new_gu, new_dn = move_weights_after(new_gu, new_dn, partner)
    gate_mean, gate_square, down_mean, down_square = move_moments(
        gate_mean, gate_square, down_mean, down_square, partner
    )
    return (
        in_grad,
        new_gu[None],
        new_dn[None],
        gate_mean[None],
        gate_square[None],
        down_mean[None],
        down_square[None],
    )


def solution(mesh):
    in_specs = (
        P(("dp", "expert"), None),
        P(("dp", "expert"), None),
        P(("dp", "expert"), None),
        P(("dp", "expert"), None),
        P("expert", None, None),
        P("expert", None, None),
        P("expert", "dp", None),
        P("expert", "dp", None),
        P("expert", None, "dp"),
        P("expert", None, "dp"),
        P(),
    )
    out_specs = (
        P(("dp", "expert"), None),
        P("expert", "dp", None),
        P("expert", None, "dp"),
        P("expert", "dp", None),
        P("expert", "dp", None),
        P("expert", None, "dp"),
        P("expert", None, "dp"),
    )
    return jax.shard_map(
        per_device, mesh=mesh, in_specs=in_specs, out_specs=out_specs, check_vma=False
    )
```

profile of v0, /device:TPU:2, one launch (start us, length us, event | category | flops | bytes accessed | tf_op | source)
XLA Modules:
  0.0 669.4 jit_solution(3657734862248697985)
XLA Ops:
  25.7 16.0 %all-to-all-start.1 = ((bf16[128,8,1024]{2,1,0:T(8,128)(2,1)}), bf16[128,8,1024]{2,1,0:T(8,128)(2,1)}, u32[]{:S(2)}, u32[]{:S(2)}) async-start(bf16[128,8,1024]{2,1,0:T(8,128)(2,1)} %bitcast_select_fusion), calls=%async_computation.1 | async-start | bytes 4194304 | tf_op jit(solution)/shard_map/all_to_all | solution.py:184
  47.7 46.3 %all-to-all-done.1 = bf16[128,8,1024]{2,1,0:T(8,128)(2,1)} async-done(((bf16[128,8,1024]{2,1,0:T(8,128)(2,1)}), bf16[128,8,1024]{2,1,0:T(8,128)(2,1)}, u32[]{:S(2)}, u32[]{:S(2)}) %all-to-all-start.1) | async-done | bytes 2097184 | tf_op jit(solution)/shard_map/all_to_all | solution.py:184
  106.9 46.3 %all-to-all-done = bf16[128,8,1024]{2,1,0:T(8,128)(2,1)S(1)} async-done(((bf16[128,8,1024]{2,1,0:T(8,128)(2,1)}), bf16[128,8,1024]{2,1,0:T(8,128)(2,1)S(1)}, u32[]{:S(2)}, u32[]{:S(2)}) %all-to-all-start) | async-done | bytes 2097184 | tf_op jit(solution)/shard_map/all_to_all | solution.py:177
  168.1 16.2 %reduce-scatter.3.cloned.1.call-done = bf16[512,768]{1,0:T(8,128)(2,1)} async-done(((bf16[1024,768]{1,0:T(8,128)(2,1)}), bf16[512,768]{1,0:T(8,128)(2,1)}) %reduce-scatter.3.cloned.1.call-update) | async-done | bytes 786448 | tf_op jit(solution)/shard_map/reduce_scatter | solution.py:211
  198.4 13.8 %all-to-all-start.5 = ((bf16[128,2,768]{2,1,0:T(2,128)(2,1)}), bf16[128,2,768]{2,1,0:T(2,128)(2,1)S(1)}, u32[]{:S(2)}, u32[]{:S(2)}) async-start(bf16[128,2,768]{2,1,0:T(2,128)(2,1)} %reshape.474), calls=%async_computation.7 | async-start | bytes 786432 | tf_op jit(solution)/shard_map/all_to_all | solution.py:126
  217.0 12.9 %all-to-all-done.5 = bf16[128,2,768]{2,1,0:T(2,128)(2,1)S(1)} async-done(((bf16[128,2,768]{2,1,0:T(2,128)(2,1)}), bf16[128,2,768]{2,1,0:T(2,128)(2,1)S(1)}, u32[]{:S(2)}, u32[]{:S(2)}) %all-to-all-start.5) | async-done | bytes 393248 | tf_op jit(solution)/shard_map/all_to_all | solution.py:126
  240.8 48.4 %all-to-all-done.2 = bf16[128,8,1024]{2,1,0:T(8,128)(2,1)S(1)} async-done(((bf16[128,8,1024]{2,1,0:T(8,128)(2,1)}), bf16[128,8,1024]{2,1,0:T(8,128)(2,1)S(1)}, u32[]{:S(2)}, u32[]{:S(2)}) %all-to-all-start.2) | async-done | bytes 2097184 | tf_op jit(solution)/shard_map/all_to_all | solution.py:198
  289.1 7.5 %all-to-all-start.13 = ((f32[1,128,1536]{2,0,1:T(1,128)}), f32[1,128,1536]{2,0,1:T(1,128)}, u32[]{:S(2)}, u32[]{:S(2)}) async-start(f32[1,128,1536]{2,0,1:T(1,128)} %reshape.460), calls=%async_computation.15 | async-start | bytes 1572864 | tf_op jit(solution)/shard_map/all_to_all | solution.py:97
  298.5 21.6 %all-to-all-done.13 = f32[1,128,1536]{2,0,1:T(1,128)} async-done(((f32[1,128,1536]{2,0,1:T(1,128)}), f32[1,128,1536]{2,0,1:T(1,128)}, u32[]{:S(2)}, u32[]{:S(2)}) %all-to-all-start.13) | async-done | bytes 786464 | tf_op jit(solution)/shard_map/all_to_all | solution.py:97
  320.0 8.0 %all-to-all-start.11 = ((f32[1,128,1536]{2,0,1:T(1,128)}), f32[1,128,1536]{2,0,1:T(1,128)}, u32[]{:S(2)}, u32[]{:S(2)}) async-start(f32[1,128,1536]{2,0,1:T(1,128)} %reshape.458), calls=%async_computation.13 | async-start | bytes 1572864 | tf_op jit(solution)/shard_map/all_to_all | solution.py:90
  350.2 10.9 %all-to-all-start.3 = ((bf16[128,2,1536]{2,1,0:T(2,128)(2,1)}), bf16[128,2,1536]{2,1,0:T(2,128)(2,1)}, u32[]{:S(2)}, u32[]{:S(2)}) async-start(bf16[128,2,1536]{2,1,0:T(2,128)(2,1)} %reshape.470), calls=%async_computation.5 | async-start | bytes 1572864 | tf_op jit(solution)/shard_map/all_to_all | solution.py:123
  364.6 18.3 %all-to-all-done.3 = bf16[128,2,1536]{2,1,0:T(2,128)(2,1)} async-done(((bf16[128,2,1536]{2,1,0:T(2,128)(2,1)}), bf16[128,2,1536]{2,1,0:T(2,128)(2,1)}, u32[]{:S(2)}, u32[]{:S(2)}) %all-to-all-start.3) | async-done | bytes 786464 | tf_op jit(solution)/shard_map/all_to_all | solution.py:123
  382.8 7.9 %all-to-all-start.6 = ((bf16[128,2,768]{2,1,0:T(2,128)(2,1)}), bf16[128,2,768]{2,1,0:T(2,128)(2,1)}, u32[]{:S(2)}, u32[]{:S(2)}) async-start(bf16[128,2,768]{2,1,0:T(2,128)(2,1)} %reshape.476), calls=%async_computation.8 | async-start | bytes 786432 | tf_op jit(solution)/shard_map/all_to_all | solution.py:137
  405.1 8.8 %all-to-all-start.14 = ((f32[128,1,1536]{2,1,0:T(1,128)}), f32[128,1,1536]{2,1,0:T(1,128)}, u32[]{:S(2)}, u32[]{:S(2)}) async-start(f32[128,1,1536]{2,1,0:T(1,128)} %copy.77), calls=%async_computation.16 | async-start | bytes 1572864 | tf_op jit(solution)/shard_map/all_to_all | solution.py:110
  416.9 16.9 %all-to-all-done.14 = f32[128,1,1536]{2,1,0:T(1,128)} async-done(((f32[128,1,1536]{2,1,0:T(1,128)}), f32[128,1,1536]{2,1,0:T(1,128)}, u32[]{:S(2)}, u32[]{:S(2)}) %all-to-all-start.14) | async-done | bytes 786464 | tf_op jit(solution)/shard_map/all_to_all | solution.py:110
  433.8 7.7 %all-to-all-start.12 = ((f32[128,1,1536]{2,1,0:T(1,128)}), f32[128,1,1536]{2,1,0:T(1,128)}, u32[]{:S(2)}, u32[]{:S(2)}) async-start(f32[128,1,1536]{2,1,0:T(1,128)} %copy.75), calls=%async_computation.14 | async-start | bytes 1572864 | tf_op jit(solution)/shard_map/all_to_all | solution.py:109
  444.2 16.0 %all-to-all-done.12 = f32[128,1,1536]{2,1,0:T(1,128)} async-done(((f32[128,1,1536]{2,1,0:T(1,128)}), f32[128,1,1536]{2,1,0:T(1,128)}, u32[]{:S(2)}, u32[]{:S(2)}) %all-to-all-start.12) | async-done | bytes 786464 | tf_op jit(solution)/shard_map/all_to_all | solution.py:109
  470.2 31.2 %all-to-all-done.9 = f32[1,128,3072]{2,0,1:T(1,128)S(1)} async-done(((f32[1,128,3072]{2,0,1:T(1,128)}), f32[1,128,3072]{2,0,1:T(1,128)S(1)}, u32[]{:S(2)}, u32[]{:S(2)}) %all-to-all-start.9) | async-done | bytes 1572896 | tf_op jit(solution)/shard_map/all_to_all | solution.py:83
  520.3 23.0 %all-to-all-done.7 = f32[1,128,3072]{2,0,1:T(1,128)} async-done(((f32[1,128,3072]{2,0,1:T(1,128)}), f32[1,128,3072]{2,0,1:T(1,128)}, u32[]{:S(2)}, u32[]{:S(2)}) %all-to-all-start.7) | async-done | bytes 1572896 | tf_op jit(solution)/shard_map/all_to_all | solution.py:76
  543.4 7.5 %all-to-all-start.4 = ((bf16[128,2,1536]{2,1,0:T(2,128)(2,1)}), bf16[128,2,1536]{2,1,0:T(2,128)(2,1)}, u32[]{:S(2)}, u32[]{:S(2)}) async-start(bf16[128,2,1536]{2,1,0:T(2,128)(2,1)} %reshape.472), calls=%async_computation.6 | async-start | bytes 1572864 | tf_op jit(solution)/shard_map/all_to_all | solution.py:136
  560.9 9.3 %all-to-all-done.4 = bf16[128,2,1536]{2,1,0:T(2,128)(2,1)} async-done(((bf16[128,2,1536]{2,1,0:T(2,128)(2,1)}), bf16[128,2,1536]{2,1,0:T(2,128)(2,1)}, u32[]{:S(2)}, u32[]{:S(2)}) %all-to-all-start.4) | async-done | bytes 786464 | tf_op jit(solution)/shard_map/all_to_all | solution.py:136
  570.2 7.9 %all-to-all-start.10 = ((f32[128,1,3072]{2,1,0:T(1,128)}), f32[128,1,3072]{2,1,0:T(1,128)}, u32[]{:S(2)}, u32[]{:S(2)}) async-start(f32[128,1,3072]{2,1,0:T(1,128)} %copy.73), calls=%async_computation.12 | async-start | bytes 3145728 | tf_op jit(solution)/shard_map/all_to_all | solution.py:108
  580.8 31.5 %all-to-all-done.10 = f32[128,1,3072]{2,1,0:T(1,128)} async-done(((f32[128,1,3072]{2,1,0:T(1,128)}), f32[128,1,3072]{2,1,0:T(1,128)}, u32[]{:S(2)}, u32[]{:S(2)}) %all-to-all-start.10) | async-done | bytes 1572896 | tf_op jit(solution)/shard_map/all_to_all | solution.py:108
  612.3 7.5 %all-to-all-start.8 = ((f32[128,1,3072]{2,1,0:T(1,128)}), f32[128,1,3072]{2,1,0:T(1,128)}, u32[]{:S(2)}, u32[]{:S(2)}) async-start(f32[128,1,3072]{2,1,0:T(1,128)} %copy.71), calls=%async_computation.10 | async-start | bytes 3145728 | tf_op jit(solution)/shard_map/all_to_all | solution.py:107
  (144 shorter events, 211.0 us)
Async XLA Ops:
  25.7 68.3 %all-to-all-start.1 = ((bf16[128,8,1024]{2,1,0:T(8,128)(2,1)}), bf16[128,8,1024]{2,1,0:T(8,128)(2,1)}, u32[]{:S(2)}, u32[]{:S(2)}) async-start(bf16[128,8,1024]{2,1,0:T(8,128)(2,1)} %bitcast_select_fusion), calls=%async_computation.1 | async-start | bytes 4194304 | tf_op jit(solution)/shard_map/all_to_all | solution.py:184
  94.0 59.1 %all-to-all-start = ((bf16[128,8,1024]{2,1,0:T(8,128)(2,1)}), bf16[128,8,1024]{2,1,0:T(8,128)(2,1)S(1)}, u32[]{:S(2)}, u32[]{:S(2)}) async-start(bf16[128,8,1024]{2,1,0:T(8,128)(2,1)} %fusion), calls=%async_computation | async-start | bytes 4194304 | tf_op jit(solution)/shard_map/all_to_all | solution.py:177
  101.3 65.1 %reduce-scatter.5.cloned.1.call-start = ((), (), s32[]{:S(2)}) async-start(), calls=%async_computation.18 | async-start | bytes 1179648 | tf_op jit(solution)/shard_map/reduce_scatter | solution.py:214
  106.9 50.3 %copy-start.11 = (bf16[1,384,1024]{2,1,0:T(8,128)(2,1)S(1)}, bf16[1,384,1024]{2,1,0:T(8,128)(2,1)}, u32[]{:S(2)}) copy-start(bf16[1,384,1024]{2,1,0:T(8,128)(2,1)} %param.20) | copy-start | bytes 2359300
  156.9 27.4 %reduce-scatter.3.cloned.1.call-start = ((), (), s32[]{:S(2)}) async-start(), calls=%async_computation.17 | async-start | bytes 2359296 | tf_op jit(solution)/shard_map/reduce_scatter | solution.py:211
  166.3 24.9 %copy-start.9 = (f32[1,384,512]{2,1,0:T(8,128)S(1)}, f32[1,384,512]{2,1,0:T(8,128)}, u32[]{:S(2)}) copy-start(f32[1,384,512]{2,1,0:T(8,128)} %param.24) | copy-start | bytes 2359300
  166.3 24.9 %copy-start.10 = (f32[1,384,512]{2,1,0:T(8,128)S(1)}, f32[1,384,512]{2,1,0:T(8,128)}, u32[]{:S(2)}) copy-start(f32[1,384,512]{2,1,0:T(8,128)} %param.23) | copy-start | bytes 2359300
  194.0 18.1 %copy-start.14 = (bf16[1024,384]{0,1:T(8,128)(2,1)S(1)}, bf16[1024,384]{0,1:T(8,128)(2,1)}, u32[]{:S(2)}) copy-start(bf16[1024,384]{0,1:T(8,128)(2,1)} %copy-done.13) | copy-start | bytes 2359300
  198.4 31.6 %all-to-all-start.5 = ((bf16[128,2,768]{2,1,0:T(2,128)(2,1)}), bf16[128,2,768]{2,1,0:T(2,128)(2,1)S(1)}, u32[]{:S(2)}, u32[]{:S(2)}) async-start(bf16[128,2,768]{2,1,0:T(2,128)(2,1)} %reshape.474), calls=%async_computation.7 | async-start | bytes 786432 | tf_op jit(solution)/shard_map/all_to_all | solution.py:126
  230.7 58.4 %all-to-all-start.2 = ((bf16[128,8,1024]{2,1,0:T(8,128)(2,1)}), bf16[128,8,1024]{2,1,0:T(8,128)(2,1)S(1)}, u32[]{:S(2)}, u32[]{:S(2)}) async-start(bf16[128,8,1024]{2,1,0:T(8,128)(2,1)} %convert_bitcast_fusion), calls=%async_computation.2 | async-start | bytes 4194304 | tf_op jit(solution)/shard_map/all_to_all | solution.py:198
  289.1 30.9 %all-to-all-start.13 = ((f32[1,128,1536]{2,0,1:T(1,128)}), f32[1,128,1536]{2,0,1:T(1,128)}, u32[]{:S(2)}, u32[]{:S(2)}) async-start(f32[1,128,1536]{2,0,1:T(1,128)} %reshape.460), calls=%async_computation.15 | async-start | bytes 1572864 | tf_op jit(solution)/shard_map/all_to_all | solution.py:97
  298.5 29.6 %copy-start.6 = (bf16[512,768]{1,0:T(8,128)(2,1)S(1)}, bf16[512,768]{1,0:T(8,128)(2,1)}, u32[]{:S(2)}) copy-start(bf16[512,768]{1,0:T(8,128)(2,1)} %reduce-scatter.3.cloned.1.call-done) | copy-start | bytes 2359300
  320.0 30.2 %all-to-all-start.11 = ((f32[1,128,1536]{2,0,1:T(1,128)}), f32[1,128,1536]{2,0,1:T(1,128)}, u32[]{:S(2)}, u32[]{:S(2)}) async-start(f32[1,128,1536]{2,0,1:T(1,128)} %reshape.458), calls=%async_computation.13 | async-start | bytes 1572864 | tf_op jit(solution)/shard_map/all_to_all | solution.py:90
  350.2 32.6 %all-to-all-start.3 = ((bf16[128,2,1536]{2,1,0:T(2,128)(2,1)}), bf16[128,2,1536]{2,1,0:T(2,128)(2,1)}, u32[]{:S(2)}, u32[]{:S(2)}) async-start(bf16[128,2,1536]{2,1,0:T(2,128)(2,1)} %reshape.470), calls=%async_computation.5 | async-start | bytes 1572864 | tf_op jit(solution)/shard_map/all_to_all | solution.py:123
  382.8 22.2 %all-to-all-start.6 = ((bf16[128,2,768]{2,1,0:T(2,128)(2,1)}), bf16[128,2,768]{2,1,0:T(2,128)(2,1)}, u32[]{:S(2)}, u32[]{:S(2)}) async-start(bf16[128,2,768]{2,1,0:T(2,128)(2,1)} %reshape.476), calls=%async_computation.8 | async-start | bytes 786432 | tf_op jit(solution)/shard_map/all_to_all | solution.py:137
  405.1 28.7 %all-to-all-start.14 = ((f32[128,1,1536]{2,1,0:T(1,128)}), f32[128,1,1536]{2,1,0:T(1,128)}, u32[]{:S(2)}, u32[]{:S(2)}) async-start(f32[128,1,1536]{2,1,0:T(1,128)} %copy.77), calls=%async_computation.16 | async-start | bytes 1572864 | tf_op jit(solution)/shard_map/all_to_all | solution.py:110
  413.9 27.6 %copy-start.5 = (f32[512,768]{1,0:T(8,128)S(1)}, f32[512,768]{1,0:T(8,128)}, u32[]{:S(2)}) copy-start(f32[512,768]{1,0:T(8,128)} %get-tuple-element.15) | copy-start | bytes 4718596
  433.8 26.4 %all-to-all-start.12 = ((f32[128,1,1536]{2,1,0:T(1,128)}), f32[128,1,1536]{2,1,0:T(1,128)}, u32[]{:S(2)}, u32[]{:S(2)}) async-start(f32[128,1,1536]{2,1,0:T(1,128)} %copy.75), calls=%async_computation.14 | async-start | bytes 1572864 | tf_op jit(solution)/shard_map/all_to_all | solution.py:109
  460.2 41.2 %all-to-all-start.9 = ((f32[1,128,3072]{2,0,1:T(1,128)}), f32[1,128,3072]{2,0,1:T(1,128)S(1)}, u32[]{:S(2)}, u32[]{:S(2)}) async-start(f32[1,128,3072]{2,0,1:T(1,128)} %reshape.456), calls=%async_computation.11 | async-start | bytes 3145728 | tf_op jit(solution)/shard_map/all_to_all | solution.py:83
  501.4 42.0 %all-to-all-start.7 = ((f32[1,128,3072]{2,0,1:T(1,128)}), f32[1,128,3072]{2,0,1:T(1,128)}, u32[]{:S(2)}, u32[]{:S(2)}) async-start(f32[1,128,3072]{2,0,1:T(1,128)} %reshape.454), calls=%async_computation.9 | async-start | bytes 3145728 | tf_op jit(solution)/shard_map/all_to_all | solution.py:76
  543.4 26.8 %all-to-all-start.4 = ((bf16[128,2,1536]{2,1,0:T(2,128)(2,1)}), bf16[128,2,1536]{2,1,0:T(2,128)(2,1)}, u32[]{:S(2)}, u32[]{:S(2)}) async-start(bf16[128,2,1536]{2,1,0:T(2,128)(2,1)} %reshape.472), calls=%async_computation.6 | async-start | bytes 1572864 | tf_op jit(solution)/shard_map/all_to_all | solution.py:136
  570.2 42.1 %all-to-all-start.10 = ((f32[128,1,3072]{2,1,0:T(1,128)}), f32[128,1,3072]{2,1,0:T(1,128)}, u32[]{:S(2)}, u32[]{:S(2)}) async-start(f32[128,1,3072]{2,1,0:T(1,128)} %copy.73), calls=%async_computation.12 | async-start | bytes 3145728 | tf_op jit(solution)/shard_map/all_to_all | solution.py:108
  580.8 39.0 %copy-start.4 = (bf16[128,8,1024]{2,1,0:T(8,128)(2,1)S(1)}, bf16[128,8,1024]{2,1,0:T(8,128)(2,1)}, u32[]{:S(2)}) copy-start(bf16[128,8,1024]{2,1,0:T(8,128)(2,1)} %copy-done.3) | copy-start | bytes 6291460
  612.3 43.1 %all-to-all-start.8 = ((f32[128,1,3072]{2,1,0:T(1,128)}), f32[128,1,3072]{2,1,0:T(1,128)}, u32[]{:S(2)}, u32[]{:S(2)}) async-start(f32[128,1,3072]{2,1,0:T(1,128)} %copy.71), calls=%async_computation.10 | async-start | bytes 3145728 | tf_op jit(solution)/shard_map/all_to_all | solution.py:107
  (9 other events, 83.2 us)
Sparse Core Ops, SparseCore 0:
  157.1 8.2 reduce-scatter.4
  168.6 15.7 reduce-scatter.2
where the time goes:
time: 679 us; the launch traced here: 669 us
  waiting for transfers between devices  347 us (51%)
  starting transfers between devices  133 us (20%)
  local copies, waits for them, and re-layouts  91.6 us (13%)
  other arithmetic  56.2 us (8%)
  matrix products  22.1 us (3%)
  between operations  17 us (3%)
    all_to_all x1, waiting for transfers between devices, per_device(): lax.all_to_all(slot_back.reshape(expert_count, capacity, model_width), 'e...  48.4 us
    all_to_all x1, waiting for transfers between devices, per_device(): lax.all_to_all(slot_input.reshape(expert_count, capacity, model_width), '...  46.3 us
    all_to_all x1, waiting for transfers between devices, per_device(): lax.all_to_all(slot_grad.reshape(expert_count, capacity, model_width), 'e...  46.3 us
    all_to_all x1, waiting for transfers between devices, move_moments(): lax.all_to_all(picked[1], 'expert', split_axis=0, concat_axis=1, tiled=True)  31.5 us
    all_to_all x1, waiting for transfers between devices, move_moments(): lax.all_to_all(gate_square.reshape(1, expert_count, -1), 'expert', split_...  31.2 us
    unnamed x50, local copies, waits for them, and re-layouts  30.7 us
    all_to_all x1, waiting for transfers between devices, move_moments(): lax.all_to_all(gate_mean.reshape(1, expert_count, -1), 'expert', split_ax...  23 us
    all_to_all x1, waiting for transfers between devices, move_moments(): lax.all_to_all(down_square.reshape(1, expert_count, -1), 'expert', split_...  21.6 us
  transfers between devices with their start and end apart: 17, of which 15 were waited for; matrix products, arithmetic and copies ran while one was open for 19% of the time, Pallas kernels for 0%

commit v1 on v0

--- a/solution.py
+++ b/solution.py
@@ -9,6 +9,12 @@
 DECAY = 0.1
 ADAM_EPS = 1e-08
 PEAK_EPS = 1e-06
+
+
+def exchange_blocks(x, axis, split, join):
+    pieces = jnp.split(x, lax.axis_size(axis), axis=split)
+    incoming = lax.all_to_all(jnp.stack(pieces), axis, 0, 0)
+    return jnp.concatenate(incoming, axis=join)
 
 
 def partner_table(swap_pairs, expert_count):
@@ -73,13 +79,7 @@
 def move_moments(gate_mean, gate_square, down_mean, down_square, partner):
     expert_count = partner.shape[0]
     spread_out = (
-        lax.all_to_all(
-            gate_mean.reshape(1, expert_count, -1),
-            "expert",
-            split_axis=1,
-            concat_axis=0,
-            tiled=True,
-        ),
+        exchange_blocks(gate_mean.reshape(1, expert_count, -1), "expert", 1, 0),
         lax.all_to_all(
             gate_square.reshape(1, expert_count, -1),
             "expert",

time: 679 us -> 757 us (1.11)
  local copies, waits for them, and re-layouts: 91.6 us -> 178 us
    unnamed x50 -> x193, local copies, waits for them, and re-layouts: 30.7 us -> 124 us
    all_to_all x1, waiting for transfers between devices: 12.9 us -> 0.01 us  [move_weights_after(): lax.all_to_all(down_proj.reshape(1, expert_count, -1), 'expert', split_ax...]
    all_to_all x1, waiting for transfers between devices: 23 us -> 34.4 us  [exchange_blocks(): incoming = lax.all_to_all(jnp.stack(pieces), axis, 0, 0)]
    all_to_all x1, waiting for transfers between devices: 48.4 us -> 39.1 us  [per_device(): lax.all_to_all(slot_back.reshape(expert_count, capacity, model_width), 'e...]
    all_to_all x1, waiting for transfers between devices: 3.34 us -> 11.4 us  [move_moments(): lax.all_to_all(down_mean.reshape(1, expert_count, -1), 'expert', split_ax...]
  transfers between devices with their start and end apart: 17 -> 17, of which waited for: 15 -> 15; matrix products, arithmetic and copies ran while one was open for 19% -> 28% of each run, Pallas kernels for 0% -> 0%
where the time goes in v1:
time: 757 us; the launch traced here: 746 us
  waiting for transfers between devices  342 us (45%)
  local copies, waits for them, and re-layouts  178 us (24%)
  starting transfers between devices  133 us (18%)
  other arithmetic  50.8 us (7%)
  matrix products  22.4 us (3%)
  between operations  17.1 us (2%)
    unnamed x193, local copies, waits for them, and re-layouts  124 us
    all_to_all x1, waiting for transfers between devices, per_device(): lax.all_to_all(slot_grad.reshape(expert_count, capacity, model_width), 'e...  46.3 us
    all_to_all x1, waiting for transfers between devices, per_device(): lax.all_to_all(slot_input.reshape(expert_count, capacity, model_width), '...  46.3 us
    all_to_all x1, waiting for transfers between devices, per_device(): lax.all_to_all(slot_back.reshape(expert_count, capacity, model_width), 'e...  39.1 us
    all_to_all x1, waiting for transfers between devices, exchange_blocks(): incoming = lax.all_to_all(jnp.stack(pieces), axis, 0, 0)  34.4 us
    all_to_all x1, waiting for transfers between devices, move_moments(): lax.all_to_all(picked[1], 'expert', split_axis=0, concat_axis=1, tiled=True)  33.3 us
    all_to_all x1, waiting for transfers between devices, move_moments(): lax.all_to_all(gate_square.reshape(1, expert_count, -1), 'expert', split_...  29.2 us
    all_to_all x1, waiting for transfers between devices, move_moments(): lax.all_to_all(down_square.reshape(1, expert_count, -1), 'expert', split_...  17.9 us
  transfers between devices with their start and end apart: 17, of which 15 were waited for; matrix products, arithmetic and copies ran while one was open for 28% of the time, Pallas kernels for 0%

profile of v1, /device:TPU:2, one launch (start us, length us, event | category | flops | bytes accessed | tf_op | source)
XLA Modules:
  0.0 746.1 jit_solution(8509542572352011516)
XLA Ops:
  26.6 16.0 %all-to-all-start.1 = ((bf16[128,8,1024]{2,1,0:T(8,128)(2,1)}), bf16[128,8,1024]{2,1,0:T(8,128)(2,1)}, u32[]{:S(2)}, u32[]{:S(2)}) async-start(bf16[128,8,1024]{2,1,0:T(8,128)(2,1)} %bitcast_select_fusion), calls=%async_computation.1 | async-start | bytes 4194304 | tf_op jit(solution)/shard_map/all_to_all | solution.py:184
  48.6 46.3 %all-to-all-done.1 = bf16[128,8,1024]{2,1,0:T(8,128)(2,1)} async-done(((bf16[128,8,1024]{2,1,0:T(8,128)(2,1)}), bf16[128,8,1024]{2,1,0:T(8,128)(2,1)}, u32[]{:S(2)}, u32[]{:S(2)}) %all-to-all-start.1) | async-done | bytes 2097184 | tf_op jit(solution)/shard_map/all_to_all | solution.py:184
  94.9 7.2 all-to-all-start
  107.7 46.3 %all-to-all-done = bf16[128,8,1024]{2,1,0:T(8,128)(2,1)S(1)} async-done(((bf16[128,8,1024]{2,1,0:T(8,128)(2,1)}), bf16[128,8,1024]{2,1,0:T(8,128)(2,1)S(1)}, u32[]{:S(2)}, u32[]{:S(2)}) %all-to-all-start) | async-done | bytes 2097184 | tf_op jit(solution)/shard_map/all_to_all | solution.py:177
  168.9 16.3 %reduce-scatter.3.cloned.1.call-done = bf16[512,768]{1,0:T(8,128)(2,1)} async-done(((bf16[1024,768]{1,0:T(8,128)(2,1)}), bf16[512,768]{1,0:T(8,128)(2,1)}) %reduce-scatter.3.cloned.1.call-update) | async-done | bytes 786448 | tf_op jit(solution)/shard_map/reduce_scatter | solution.py:211
  203.6 14.8 %all-to-all-start.5 = ((bf16[128,2,768]{2,1,0:T(2,128)(2,1)}), bf16[128,2,768]{2,1,0:T(2,128)(2,1)}, u32[]{:S(2)}, u32[]{:S(2)}) async-start(bf16[128,2,768]{2,1,0:T(2,128)(2,1)} %reshape.474), calls=%async_computation.7 | async-start | bytes 786432 | tf_op jit(solution)/shard_map/all_to_all | solution.py:126
  288.1 13.7 %all-to-all-start.2 = ((bf16[128,8,1024]{2,1,0:T(8,128)(2,1)}), bf16[128,8,1024]{2,1,0:T(8,128)(2,1)S(1)}, u32[]{:S(2)}, u32[]{:S(2)}) async-start(bf16[128,8,1024]{2,1,0:T(8,128)(2,1)} %convert_bitcast_fusion), calls=%async_computation.2 | async-start | bytes 4194304 | tf_op jit(solution)/shard_map/all_to_all | solution.py:198
  315.4 39.1 %all-to-all-done.2 = bf16[128,8,1024]{2,1,0:T(8,128)(2,1)S(1)} async-done(((bf16[128,8,1024]{2,1,0:T(8,128)(2,1)}), bf16[128,8,1024]{2,1,0:T(8,128)(2,1)S(1)}, u32[]{:S(2)}, u32[]{:S(2)}) %all-to-all-start.2) | async-done | bytes 2097184 | tf_op jit(solution)/shard_map/all_to_all | solution.py:198
  354.5 7.6 %all-to-all-start.13 = ((f32[1,128,1536]{2,0,1:T(1,128)}), f32[1,128,1536]{2,0,1:T(1,128)}, u32[]{:S(2)}, u32[]{:S(2)}) async-start(f32[1,128,1536]{2,0,1:T(1,128)} %reshape.460), calls=%async_computation.15 | async-start | bytes 1572864 | tf_op jit(solution)/shard_map/all_to_all | solution.py:97
  368.4 17.9 %all-to-all-done.13 = f32[1,128,1536]{2,0,1:T(1,128)} async-done(((f32[1,128,1536]{2,0,1:T(1,128)}), f32[1,128,1536]{2,0,1:T(1,128)}, u32[]{:S(2)}, u32[]{:S(2)}) %all-to-all-start.13) | async-done | bytes 786464 | tf_op jit(solution)/shard_map/all_to_all | solution.py:97
  386.3 8.0 %all-to-all-start.11 = ((f32[1,128,1536]{2,0,1:T(1,128)}), f32[1,128,1536]{2,0,1:T(1,128)}, u32[]{:S(2)}, u32[]{:S(2)}) async-start(f32[1,128,1536]{2,0,1:T(1,128)} %reshape.458), calls=%async_computation.13 | async-start | bytes 1572864 | tf_op jit(solution)/shard_map/all_to_all | solution.py:90
  406.0 11.4 %all-to-all-done.11 = f32[1,128,1536]{2,0,1:T(1,128)} async-done(((f32[1,128,1536]{2,0,1:T(1,128)}), f32[1,128,1536]{2,0,1:T(1,128)}, u32[]{:S(2)}, u32[]{:S(2)}) %all-to-all-start.11) | async-done | bytes 786464 | tf_op jit(solution)/shard_map/all_to_all | solution.py:90
  432.3 14.6 %all-to-all-done.3 = bf16[128,2,1536]{2,1,0:T(2,128)(2,1)S(1)} async-done(((bf16[128,2,1536]{2,1,0:T(2,128)(2,1)}), bf16[128,2,1536]{2,1,0:T(2,128)(2,1)S(1)}, u32[]{:S(2)}, u32[]{:S(2)}) %all-to-all-start.3) | async-done | bytes 786464 | tf_op jit(solution)/shard_map/all_to_all | solution.py:123
  468.5 7.7 %all-to-all-start.14 = ((f32[128,1,1536]{2,1,0:T(1,128)}), f32[128,1,1536]{2,1,0:T(1,128)S(1)}, u32[]{:S(2)}, u32[]{:S(2)}) async-start(f32[128,1,1536]{2,1,0:T(1,128)} %copy.74), calls=%async_computation.16 | async-start | bytes 1572864 | tf_op jit(solution)/shard_map/all_to_all | solution.py:110
  482.4 15.8 %all-to-all-done.14 = f32[128,1,1536]{2,1,0:T(1,128)S(1)} async-done(((f32[128,1,1536]{2,1,0:T(1,128)}), f32[128,1,1536]{2,1,0:T(1,128)S(1)}, u32[]{:S(2)}, u32[]{:S(2)}) %all-to-all-start.14) | async-done | bytes 786464 | tf_op jit(solution)/shard_map/all_to_all | solution.py:110
  509.4 17.1 %all-to-all-done.12 = f32[128,1,1536]{2,1,0:T(1,128)S(1)} async-done(((f32[128,1,1536]{2,1,0:T(1,128)}), f32[128,1,1536]{2,1,0:T(1,128)S(1)}, u32[]{:S(2)}, u32[]{:S(2)}) %all-to-all-start.12) | async-done | bytes 786464 | tf_op jit(solution)/shard_map/all_to_all | solution.py:109
  536.8 34.4 %all-to-all-done.7 = f32[128,1,1,3072]{3,2,1,0:T(1,128)S(1)} async-done(((f32[128,1,1,3072]{3,2,1,0:T(1,128)}), f32[128,1,1,3072]{3,2,1,0:T(1,128)S(1)}, u32[]{:S(2)}, u32[]{:S(2)}) %all-to-all-start.7) | async-done | bytes 1572896 | tf_op jit(solution)/shard_map/all_to_all | solution.py:16
  571.2 7.9 %all-to-all-start.9 = ((f32[1,128,3072]{2,0,1:T(1,128)}), f32[1,128,3072]{2,0,1:T(1,128)}, u32[]{:S(2)}, u32[]{:S(2)}) async-start(f32[1,128,3072]{2,0,1:T(1,128)} %reshape.456), calls=%async_computation.11 | async-start | bytes 3145728 | tf_op jit(solution)/shard_map/all_to_all | solution.py:83
  586.6 29.2 %all-to-all-done.9 = f32[1,128,3072]{2,0,1:T(1,128)} async-done(((f32[1,128,3072]{2,0,1:T(1,128)}), f32[1,128,3072]{2,0,1:T(1,128)}, u32[]{:S(2)}, u32[]{:S(2)}) %all-to-all-start.9) | async-done | bytes 1572896 | tf_op jit(solution)/shard_map/all_to_all | solution.py:83
  615.7 7.4 all-to-all-start.4
  633.2 11.0 %all-to-all-done.4 = bf16[128,2,1536]{2,1,0:T(2,128)(2,1)} async-done(((bf16[128,2,1536]{2,1,0:T(2,128)(2,1)}), bf16[128,2,1536]{2,1,0:T(2,128)(2,1)}, u32[]{:S(2)}, u32[]{:S(2)}) %all-to-all-start.4) | async-done | bytes 786464 | tf_op jit(solution)/shard_map/all_to_all | solution.py:136
  644.2 7.7 %all-to-all-start.10 = ((f32[128,1,3072]{2,1,0:T(1,128)}), f32[128,1,3072]{2,1,0:T(1,128)}, u32[]{:S(2)}, u32[]{:S(2)}) async-start(f32[128,1,3072]{2,1,0:T(1,128)} %copy.70), calls=%async_computation.12 | async-start | bytes 3145728 | tf_op jit(solution)/shard_map/all_to_all | solution.py:108
  654.6 33.3 %all-to-all-done.10 = f32[128,1,3072]{2,1,0:T(1,128)} async-done(((f32[128,1,3072]{2,1,0:T(1,128)}), f32[128,1,3072]{2,1,0:T(1,128)}, u32[]{:S(2)}, u32[]{:S(2)}) %all-to-all-start.10) | async-done | bytes 1572896 | tf_op jit(solution)/shard_map/all_to_all | solution.py:108
  687.9 7.6 %all-to-all-start.8 = ((f32[128,1,3072]{2,1,0:T(1,128)}), f32[128,1,3072]{2,1,0:T(1,128)}, u32[]{:S(2)}, u32[]{:S(2)}) async-start(f32[128,1,3072]{2,1,0:T(1,128)} %copy.68), calls=%async_computation.10 | async-start | bytes 3145728 | tf_op jit(solution)/shard_map/all_to_all | solution.py:107
  (287 shorter events, 290.6 us)
Async XLA Ops:
  26.6 68.3 %all-to-all-start.1 = ((bf16[128,8,1024]{2,1,0:T(8,128)(2,1)}), bf16[128,8,1024]{2,1,0:T(8,128)(2,1)}, u32[]{:S(2)}, u32[]{:S(2)}) async-start(bf16[128,8,1024]{2,1,0:T(8,128)(2,1)} %bitcast_select_fusion), calls=%async_computation.1 | async-start | bytes 4194304 | tf_op jit(solution)/shard_map/all_to_all | solution.py:184
  94.9 59.1 %all-to-all-start = ((bf16[128,8,1024]{2,1,0:T(8,128)(2,1)}), bf16[128,8,1024]{2,1,0:T(8,128)(2,1)S(1)}, u32[]{:S(2)}, u32[]{:S(2)}) async-start(bf16[128,8,1024]{2,1,0:T(8,128)(2,1)} %fusion), calls=%async_computation | async-start | bytes 4194304 | tf_op jit(solution)/shard_map/all_to_all | solution.py:177
  102.2 65.1 %reduce-scatter.5.cloned.1.call-start = ((), (), s32[]{:S(2)}) async-start(), calls=%async_computation.18 | async-start | bytes 1179648 | tf_op jit(solution)/shard_map/reduce_scatter | solution.py:214
  107.7 50.4 %copy-start.21 = (bf16[1,384,1024]{2,1,0:T(8,128)(2,1)S(1)}, bf16[1,384,1024]{2,1,0:T(8,128)(2,1)}, u32[]{:S(2)}) copy-start(bf16[1,384,1024]{2,1,0:T(8,128)(2,1)} %param.20) | copy-start | bytes 2359300
  157.8 27.4 %reduce-scatter.3.cloned.1.call-start = ((), (), s32[]{:S(2)}) async-start(), calls=%async_computation.17 | async-start | bytes 2359296 | tf_op jit(solution)/shard_map/reduce_scatter | solution.py:211
  203.6 84.5 %all-to-all-start.5 = ((bf16[128,2,768]{2,1,0:T(2,128)(2,1)}), bf16[128,2,768]{2,1,0:T(2,128)(2,1)}, u32[]{:S(2)}, u32[]{:S(2)}) async-start(bf16[128,2,768]{2,1,0:T(2,128)(2,1)} %reshape.474), calls=%async_computation.7 | async-start | bytes 786432 | tf_op jit(solution)/shard_map/all_to_all | solution.py:126
  223.6 64.5 %copy-start.5 = (f32[1,128,3072]{2,1,0:T(8,128)}, f32[1,128,3072]{2,1,0:T(8,128)S(1)}, u32[]{:S(2)}) copy-start(f32[1,128,3072]{2,1,0:T(8,128)S(1)} %reshape.320) | copy-start | bytes 4718596
  288.1 66.4 %all-to-all-start.2 = ((bf16[128,8,1024]{2,1,0:T(8,128)(2,1)}), bf16[128,8,1024]{2,1,0:T(8,128)(2,1)S(1)}, u32[]{:S(2)}, u32[]{:S(2)}) async-start(bf16[128,8,1024]{2,1,0:T(8,128)(2,1)} %convert_bitcast_fusion), calls=%async_computation.2 | async-start | bytes 4194304 | tf_op jit(solution)/shard_map/all_to_all | solution.py:198
  303.4 60.2 %copy-start.7 = (f32[384,512]{1,0:T(8,128)S(1)}, f32[384,512]{1,0:T(8,128)}, u32[]{:S(2)}) copy-start(f32[384,512]{1,0:T(8,128)} %get-tuple-element.11) | copy-start | bytes 2359300
  354.5 31.9 %all-to-all-start.13 = ((f32[1,128,1536]{2,0,1:T(1,128)}), f32[1,128,1536]{2,0,1:T(1,128)}, u32[]{:S(2)}, u32[]{:S(2)}) async-start(f32[1,128,1536]{2,0,1:T(1,128)} %reshape.460), calls=%async_computation.15 | async-start | bytes 1572864 | tf_op jit(solution)/shard_map/all_to_all | solution.py:97
  365.4 30.5 %copy-start.8 = (bf16[512,768]{1,0:T(8,128)(2,1)S(1)}, bf16[512,768]{1,0:T(8,128)(2,1)}, u32[]{:S(2)}) copy-start(bf16[512,768]{1,0:T(8,128)(2,1)} %get-tuple-element.14) | copy-start | bytes 2359300
  386.3 31.1 %all-to-all-start.11 = ((f32[1,128,1536]{2,0,1:T(1,128)}), f32[1,128,1536]{2,0,1:T(1,128)}, u32[]{:S(2)}, u32[]{:S(2)}) async-start(f32[1,128,1536]{2,0,1:T(1,128)} %reshape.458), calls=%async_computation.13 | async-start | bytes 1572864 | tf_op jit(solution)/shard_map/all_to_all | solution.py:90
  417.4 29.5 %all-to-all-start.3 = ((bf16[128,2,1536]{2,1,0:T(2,128)(2,1)}), bf16[128,2,1536]{2,1,0:T(2,128)(2,1)S(1)}, u32[]{:S(2)}, u32[]{:S(2)}) async-start(bf16[128,2,1536]{2,1,0:T(2,128)(2,1)} %reshape.470), calls=%async_computation.5 | async-start | bytes 1572864 | tf_op jit(solution)/shard_map/all_to_all | solution.py:123
  446.9 21.6 %all-to-all-start.6 = ((bf16[128,2,768]{2,1,0:T(2,128)(2,1)}), bf16[128,2,768]{2,1,0:T(2,128)(2,1)S(1)}, u32[]{:S(2)}, u32[]{:S(2)}) async-start(bf16[128,2,768]{2,1,0:T(2,128)(2,1)} %reshape.476), calls=%async_computation.8 | async-start | bytes 786432 | tf_op jit(solution)/shard_map/all_to_all | solution.py:137
  468.5 29.7 %all-to-all-start.14 = ((f32[128,1,1536]{2,1,0:T(1,128)}), f32[128,1,1536]{2,1,0:T(1,128)S(1)}, u32[]{:S(2)}, u32[]{:S(2)}) async-start(f32[128,1,1536]{2,1,0:T(1,128)} %copy.74), calls=%async_computation.16 | async-start | bytes 1572864 | tf_op jit(solution)/shard_map/all_to_all | solution.py:110
  498.2 28.3 %all-to-all-start.12 = ((f32[128,1,1536]{2,1,0:T(1,128)}), f32[128,1,1536]{2,1,0:T(1,128)S(1)}, u32[]{:S(2)}, u32[]{:S(2)}) async-start(f32[128,1,1536]{2,1,0:T(1,128)} %copy.72), calls=%async_computation.14 | async-start | bytes 1572864 | tf_op jit(solution)/shard_map/all_to_all | solution.py:109
  509.4 24.7 %copy-start.6 = (f32[512,768]{1,0:T(8,128)S(1)}, f32[512,768]{1,0:T(8,128)}, u32[]{:S(2)}) copy-start(f32[512,768]{1,0:T(8,128)} %get-tuple-element.15) | copy-start | bytes 4718596
  527.4 43.9 %all-to-all-start.7 = ((f32[128,1,1,3072]{3,2,1,0:T(1,128)}), f32[128,1,1,3072]{3,2,1,0:T(1,128)S(1)}, u32[]{:S(2)}, u32[]{:S(2)}) async-start(f32[128,1,1,3072]{3,2,1,0:T(1,128)} %constant_dynamic-update-slice_fusion), calls=%async_computation.9 | async-start | bytes 3145728 | tf_op jit(solution)/shard_map/all_to_all | solution.py:16
  536.8 42.3 %copy-start.15 = (bf16[128,2,1536]{2,1,0:T(2,128)(2,1)S(1)}, bf16[128,2,1536]{2,1,0:T(2,128)(2,1)}, u32[]{:S(2)}) copy-start(bf16[128,2,1536]{2,1,0:T(2,128)(2,1)} %copy-done.14) | copy-start | bytes 2359300
  571.2 44.5 %all-to-all-start.9 = ((f32[1,128,3072]{2,0,1:T(1,128)}), f32[1,128,3072]{2,0,1:T(1,128)}, u32[]{:S(2)}, u32[]{:S(2)}) async-start(f32[1,128,3072]{2,0,1:T(1,128)} %reshape.456), calls=%async_computation.11 | async-start | bytes 3145728 | tf_op jit(solution)/shard_map/all_to_all | solution.py:83
  615.7 28.4 %all-to-all-start.4 = ((bf16[128,2,1536]{2,1,0:T(2,128)(2,1)}), bf16[128,2,1536]{2,1,0:T(2,128)(2,1)}, u32[]{:S(2)}, u32[]{:S(2)}) async-start(bf16[128,2,1536]{2,1,0:T(2,128)(2,1)} %reshape.472), calls=%async_computation.6 | async-start | bytes 1572864 | tf_op jit(solution)/shard_map/all_to_all | solution.py:136
  644.2 43.8 %all-to-all-start.10 = ((f32[128,1,3072]{2,1,0:T(1,128)}), f32[128,1,3072]{2,1,0:T(1,128)}, u32[]{:S(2)}, u32[]{:S(2)}) async-start(f32[128,1,3072]{2,1,0:T(1,128)} %copy.70), calls=%async_computation.12 | async-start | bytes 3145728 | tf_op jit(solution)/shard_map/all_to_all | solution.py:108
  654.6 41.0 %copy-start.4 = (bf16[128,8,1024]{2,1,0:T(8,128)(2,1)S(1)}, bf16[128,8,1024]{2,1,0:T(8,128)(2,1)}, u32[]{:S(2)}) copy-start(bf16[128,8,1024]{2,1,0:T(8,128)(2,1)} %copy-done.3) | copy-start | bytes 6291460
  687.9 44.2 %all-to-all-start.8 = ((f32[128,1,3072]{2,1,0:T(1,128)}), f32[128,1,3072]{2,1,0:T(1,128)}, u32[]{:S(2)}, u32[]{:S(2)}) async-start(f32[128,1,3072]{2,1,0:T(1,128)} %copy.68), calls=%async_computation.10 | async-start | bytes 3145728 | tf_op jit(solution)/shard_map/all_to_all | solution.py:107
  (17 other events, 159.4 us)
Sparse Core Ops, SparseCore 0:
  158.0 8.2 reduce-scatter.4
  169.5 15.7 reduce-scatter.2
